TPU v7x, 256 devices: a whole 4x4x8 slice. The times are simulated.
256 devices in a mesh: grp: 32 (over x, z_lo, core), tp: 8 (over z_hi, y).
Axes of the slice: x: 4, y: 4, z: 8 (z_hi: 2, z_lo: 4; z = z_hi * 4 + z_lo), core: 2. Of those that a mesh axis runs over, the one named last changes fastest.
Arguments:
- kv_weight: bfloat16 [8192, 2048], P('tp'), may hold values from -0.0625 to 0.0625
- kv_bias: bfloat16 [2048], P('tp'), may hold values from -3 to 3
- hidden_in: bfloat16 [4, 32, 48, 8192], P(None, 'grp', None, 'tp'), may hold values from -6 to 6
- queries: bfloat16 [4, 32, 48, 8192], P(None, 'grp', None, 'tp'), may hold values from -139 to 139
- res_cache: bfloat16 [32, 16, 128, 2048], P('grp', None, None, 'tp'), may hold values from -6 to 6
- res_len: int32 [32, 16], P('grp'), may hold values from 1 to 128, 1088 in all within a row
- long_cache: bfloat16 [32, 32, 512, 2048], P('grp', None, None, 'tp'), may hold values from -6 to 6
- long_len: int32 [32, 32], replicated, may hold values from 1 to 512, 8192 in all within a row
- long_dest: int32 [32, 32], replicated, may hold values from 0 to 31, each once within a row
Outputs:
- attention_out: bfloat16 [4, 32, 48, 8192], P(None, 'grp', None, 'tp')
Inputs may be any that keep to these rules, and one draw needn't show every extreme that they name: `res_len`: each group's lengths sum to 1088, and the largest is 128. `long_len`: each home group's lengths sum to 8192, and the largest is 512. `long_dest`: each row is a permutation of the groups, so every group sends one request to every group and receives one from every group.
All inputs are finite; a program needn't handle non-finite values.
Results may differ from a plain program's by a relative error of at most 0.0051.
Values may be sent and summed in bfloat16 or wider, within the bound.
A program may use at most 128 MiB of HBM per device.

v0:
```python
import jax
import jax.numpy as jnp
from jax import lax
from jax.sharding import PartitionSpec as P

HS = 128


ROPE_BASE = 1000000.0
masked_score = -1e30


def rotate(keys_raw, positions):
    half_dim = HS // 2
    freqs = jnp.power(jnp.float32(ROPE_BASE), -2.0 * jnp.arange(half_dim, dtype=jnp.float32) / HS)
    angles = positions.astype(jnp.float32)[..., None] * freqs
    cosine = jnp.cos(angles)
    sine = jnp.sin(angles)
    first_half = keys_raw[..., :half_dim]
    second_half = keys_raw[..., half_dim:]
    return jnp.concatenate(
        [first_half * cosine - second_half * sine, second_half * cosine + first_half * sine],
        axis=-1,
    )


def attend(query, cache, lengths, new_keys, new_values):
    kv_heads = new_keys.shape[2]
    capacity = cache.shape[1]
    cache = cache.reshape(cache.shape[0], capacity, kv_heads, 2 * HS)
    old_keys = cache[..., :HS]
    old_values = cache[..., HS:]
    scale = HS ** (-0.5)
    scores_old = (
        jnp.einsum("sbkqd,bckd->sbkqc", query, old_keys, preferred_element_type=jnp.float32) * scale
    )
    valid = jnp.arange(capacity, dtype=jnp.int32)[None, :] < lengths[:, None]
    scores_old = jnp.where(valid[None, :, None, None, :], scores_old, masked_score)
    scores_new = (
        jnp.einsum("sbkqd,tbkd->sbkqt", query, new_keys, preferred_element_type=jnp.float32) * scale
    )
    step_count = new_keys.shape[0]
    causal = jnp.arange(step_count)[None, :] <= jnp.arange(step_count)[:, None]
    scores_new = jnp.where(causal[:, None, None, None, :], scores_new, masked_score)
    highest = jnp.maximum(jnp.max(scores_old, -1), jnp.max(scores_new, -1))[..., None]
    probs_old = jnp.exp(scores_old - highest)
    probs_new = jnp.exp(scores_new - highest)
    total = jnp.sum(probs_old, -1, keepdims=True) + jnp.sum(probs_new, -1, keepdims=True)
    weights_old = (probs_old / total).astype(jnp.bfloat16)
    weights_new = (probs_new / total).astype(jnp.bfloat16)
    mixed = jnp.einsum(
        "sbkqc,bckd->sbkqd", weights_old, old_values, preferred_element_type=jnp.float32
    )
    mixed = mixed + jnp.einsum(
        "sbkqt,tbkd->sbkqd", weights_new, new_values, preferred_element_type=jnp.float32
    )
    return mixed.astype(jnp.bfloat16)


def per_device(
    kv_weight, kv_bias, hidden_in, queries, res_cache, res_len, long_cache, long_len, long_dest
):
    step_count, _, serve_rows, width_part = hidden_in.shape
    kv_cols = kv_bias.shape[0]
    kv_heads = kv_cols // (2 * HS)
    head_count = queries.shape[3] // HS
    staying_count = res_cache.shape[1]
    local_weight = lax.all_to_all(kv_weight, "tp", split_axis=1, concat_axis=0, tiled=True)
    piece = lax.all_gather(hidden_in, "tp", axis=3, tiled=True)
    flat_piece = piece.reshape(step_count * serve_rows, piece.shape[3])
    kv_raw = jnp.dot(flat_piece, local_weight, preferred_element_type=jnp.float32)
    kv_raw = kv_raw + kv_bias.astype(jnp.float32)
    kv_raw = kv_raw.reshape(step_count, serve_rows, kv_heads, 2 * HS)
    group_index = lax.axis_index("grp")
    matched = (long_dest == group_index).astype(jnp.int32)
    len_in = jnp.sum(matched * long_len, axis=1)
    own_len = res_len[0]
    served_len = jnp.concatenate([own_len, len_in])
    positions = served_len[None, :] + jnp.arange(step_count, dtype=jnp.int32)[:, None]
    new_keys = rotate(kv_raw[..., :HS], positions[:, :, None]).astype(jnp.bfloat16)
    new_values = kv_raw[..., HS:].astype(jnp.bfloat16)
    query = queries[:, 0].reshape(step_count, serve_rows, kv_heads, head_count // kv_heads, HS)
    staying = attend(
        query[:, :staying_count],
        res_cache[0],
        own_len,
        new_keys[:, :staying_count],
        new_values[:, :staying_count],
    )
    own_dest = lax.dynamic_index_in_dim(long_dest, group_index, 0, keepdims=False)
    order = jnp.argsort(own_dest)
    outgoing = long_cache[0][order]
    arrived = lax.all_to_all(outgoing, "grp", split_axis=0, concat_axis=0, tiled=True)
    moving = attend(
        query[:, staying_count:],
        arrived,
        len_in,
        new_keys[:, staying_count:],
        new_values[:, staying_count:],
    )
    joined = jnp.concatenate([staying, moving], axis=1)
    return joined.reshape(step_count, 1, serve_rows, head_count * HS)


def solution(mesh):
    placed = (
        P("tp", None),
        P("tp"),
        P(None, "grp", None, "tp"),
        P(None, "grp", None, "tp"),
        P("grp", None, None, "tp"),
        P("grp", None),
        P("grp", None, None, "tp"),
        P(),
        P(),
    )
    return jax.shard_map(
        per_device,
        mesh=mesh,
        in_specs=placed,
        out_specs=P(None, "grp", None, "tp"),
        check_vma=False,
    )
```

profile of v0, /device:TPU:1, one launch (start us, length us, event | category | flops | bytes accessed | tf_op | source)
XLA Modules:
  0.0 370.8 jit_solution(15000429692429579751)
XLA Ops:
  6.5 6.4 %copy.21 = bf16[1024,2048]{0,1:T(8,128)(2,1)} copy(bf16[1024,2048]{1,0:T(8,128)(2,1)} %param.9) | data formatting | bytes 8388608 | tf_op args[0]
  12.9 11.8 %all-to-all-start = ((bf16[1024,8,256]{0,2,1:T(8,128)(2,1)}), bf16[1024,8,256]{0,2,1:T(8,128)(2,1)}, u32[]{:S(2)}, u32[]{:S(2)}) async-start(bf16[1024,8,256]{0,2,1:T(8,128)(2,1)} %bitcast.169), calls=%async_computation | async-start | bytes 8388608 | tf_op jit(solution)/shard_map/all_to_all | solution.py:68
  24.7 1.6 sort.17
  26.4 8.4 %gather_fusion = bf16[32,512,256]{2,1,0:T(8,128)(2,1)} fusion(bf16[32,512,256]{2,1,0:T(8,128)(2,1)} %bitcast.171, s32[1024]{0:T(1024)S(1)} %pad_clamp_fusion), kind=kCustom, calls=%fused_computation | custom fusion | bytes 16777344 | tf_op jit(solution)/shard_map/gather | solution.py:92
  34.8 74.6 %all-to-all-done = bf16[1024,8,256]{0,2,1:T(8,128)(2,1)} async-done(((bf16[1024,8,256]{0,2,1:T(8,128)(2,1)}), bf16[1024,8,256]{0,2,1:T(8,128)(2,1)}, u32[]{:S(2)}, u32[]{:S(2)}) %all-to-all-start) | async-done | bytes 4194336 | tf_op jit(solution)/shard_map/all_to_all | solution.py:68
  109.4 19.0 %all-to-all-start.1 = ((bf16[32,512,256]{2,1,0:T(8,128)(2,1)}), bf16[32,512,256]{2,1,0:T(8,128)(2,1)}, u32[]{:S(2)}, u32[]{:S(2)}) async-start(bf16[32,512,256]{2,1,0:T(8,128)(2,1)} %gather_fusion), calls=%async_computation.1 | async-start | bytes 16777216 | tf_op jit(solution)/shard_map/all_to_all | solution.py:93
  128.4 0.7 all-gather.2.cloned.1.call-update
  129.3 0.1 select_reduce_fusion
  129.4 0.1 pad_add_fusion
  129.5 0.1 iota_compare_fusion.1
  129.5 0.1 iota_compare_fusion
  129.7 0.5 fusion.49
  130.2 6.5 %copy.22 = bf16[8,1024,256]{2,1,0:T(8,128)(2,1)} copy(bf16[8,1024,256]{1,2,0:T(8,128)(2,1)} %bitcast.10) | data formatting | bytes 8388608 | tf_op jit(solution)/shard_map/all_to_all | solution.py:68
  136.6 109.2 %all-gather.2.cloned.1.call-done = bf16[4,1,48,8192]{3,2,1,0:T(8,128)(2,1)} async-done(((bf16[4,1,48,1024]{3,2,1,0:T(8,128)(2,1)}), bf16[4,1,48,8192]{3,2,1,0:T(8,128)(2,1)}) %all-gather.2.cloned.1.call-update) | async-done | bytes 3145744 | tf_op jit(solution)/shard_map/all_gather | solution.py:69
  245.9 4.1 %convolution_add_fusion.1 = f32[192,256]{1,0:T(8,128)S(1)} fusion(bf16[192,8192]{1,0:T(8,128)(2,1)} %bitcast.170, bf16[8192,256]{1,0:T(8,128)(2,1)} %bitcast.168, f32[256]{0:T(256)S(1)} %convert_element_type.53), kind=kOutput, calls=%fused_computation.21 | convolution fusion | flops 805355520 | bytes 7537664 | tf_op jit(solution)/shard_map/dot_general | solution.py:71
  250.0 0.1 copy.23
  250.1 0.1 copy.46
  250.3 0.8 fusion.33
  251.1 0.7 fusion.50
  251.9 0.1 fusion.31
  252.0 0.3 fusion.21
  252.3 0.3 fusion.36
  252.6 0.3 fusion.12
  252.9 1.3 fusion.48
  254.2 100.6 %all-to-all-done.1 = bf16[32,512,256]{2,1,0:T(8,128)(2,1)} async-done(((bf16[32,512,256]{2,1,0:T(8,128)(2,1)}), bf16[32,512,256]{2,1,0:T(8,128)(2,1)}, u32[]{:S(2)}, u32[]{:S(2)}) %all-to-all-start.1) | async-done | bytes 8388640 | tf_op jit(solution)/shard_map/all_to_all | solution.py:93
  354.9 3.7 %bitcast_reduce_fusion = (f32[4,32,8]{2,0,1:T(4,128)S(1)}, f32[32,512,4,8]{1,3,2,0:T(8,128)S(1)}) fusion(pred[32,512]{1,0:T(8,128)(4,1)S(1)} %iota_compare_fusion, bf16[32,512,1,256]{3,1,0,2:T(8,128)(2,1)} %bitcast.31, bf16[4,48,1,8,128]{4,3,1,0,2:T(8,128)(2,1)S(1)} %bitcast.178), kind=kOutput, calls=%fused_computation.6 | convolution fusion | flops 135789568 | bytes 6574080 | tf_op jit(solution)/shard_map/sbkqd,bckd->sbkqc/dot_general | solution.py:35
  358.6 0.8 fusion.3
  359.5 0.3 fusion.22
  359.8 2.8 fusion.1
  362.6 0.4 fusion.5
  363.0 0.1 reshape.293
  363.1 0.9 copy.26
  (27 shorter events, 0.3 us)
Async XLA Ops:
  12.9 11.8 %copy-start.1 = (s32[32,32]{1,0:T(8,128)S(1)}, s32[32,32]{1,0:T(8,128)}, u32[]{:S(2)}) copy-start(s32[32,32]{1,0:T(8,128)} %param.17) | copy-start | bytes 12292
  12.9 96.5 %all-to-all-start = ((bf16[1024,8,256]{0,2,1:T(8,128)(2,1)}), bf16[1024,8,256]{0,2,1:T(8,128)(2,1)}, u32[]{:S(2)}, u32[]{:S(2)}) async-start(bf16[1024,8,256]{0,2,1:T(8,128)(2,1)} %bitcast.169), calls=%async_computation | async-start | bytes 8388608 | tf_op jit(solution)/shard_map/all_to_all | solution.py:68
  34.8 94.4 %copy-start.5 = (bf16[256]{0:T(256)(128)(2,1)S(1)}, bf16[256]{0:T(256)(128)(2,1)}, u32[]{:S(2)}) copy-start(bf16[256]{0:T(256)(128)(2,1)} %param.10) | copy-start | bytes 1540
  34.8 94.4 %copy-start = (bf16[4,1,48,1024]{3,2,1,0:T(8,128)(2,1)S(1)}, bf16[4,1,48,1024]{3,2,1,0:T(8,128)(2,1)}, u32[]{:S(2)}) copy-start(bf16[4,1,48,1024]{3,2,1,0:T(8,128)(2,1)} %param.12) | copy-start | bytes 1179652
  34.8 94.5 %copy-start.2 = (s32[32,32]{1,0:T(8,128)S(1)}, s32[32,32]{1,0:T(8,128)}, u32[]{:S(2)}) copy-start(s32[32,32]{1,0:T(8,128)} %param.16) | copy-start | bytes 12292
  34.8 94.6 %copy-start.3 = (s32[1,16]{1,0:T(1,128)S(1)}, s32[1,16]{1,0:T(1,128)}, u32[]{:S(2)}) copy-start(s32[1,16]{1,0:T(1,128)} %param.14) | copy-start | bytes 196
  34.8 94.9 %copy-start.4 = (bf16[1,16,128,256]{3,2,1,0:T(8,128)(2,1)S(1)}, bf16[1,16,128,256]{3,2,1,0:T(8,128)(2,1)}, u32[]{:S(2)}) copy-start(bf16[1,16,128,256]{3,2,1,0:T(8,128)(2,1)} %param.13) | copy-start | bytes 3145732
  109.4 245.4 %all-to-all-start.1 = ((bf16[32,512,256]{2,1,0:T(8,128)(2,1)}), bf16[32,512,256]{2,1,0:T(8,128)(2,1)}, u32[]{:S(2)}, u32[]{:S(2)}) async-start(bf16[32,512,256]{2,1,0:T(8,128)(2,1)} %gather_fusion), calls=%async_computation.1 | async-start | bytes 16777216 | tf_op jit(solution)/shard_map/all_to_all | solution.py:93
  128.4 117.5 %all-gather.2.cloned.1.call-start = ((), (), s32[]{:S(2)}) async-start(), calls=%async_computation.2 | async-start | bytes 3538944 | tf_op jit(solution)/shard_map/all_gather | solution.py:69
Sparse Core Ops, SparseCore 0:
  131.9 113.9 all-gather.1
where the time goes:
time: 371 us
  waiting for transfers between devices  285 us (77%)
  starting transfers between devices  30.8 us (8%)
  local copies, waits for them, and re-layouts  22.6 us (6%)
  matrix products  14.2 us (4%)
  between operations  13.6 us (4%)
  other arithmetic  4.53 us (1%)
    all_gather x1, waiting for transfers between devices, per_device(): piece = lax.all_gather(hidden_in, 'tp', axis=3, tiled=True)  109 us
    all_to_all x1, waiting for transfers between devices, per_device(): lax.all_to_all(outgoing, 'grp', split_axis=0, concat_axis=0, tiled=True)  101 us
    all_to_all x1, waiting for transfers between devices, per_device(): lax.all_to_all(kv_weight, 'tp', split_axis=1, concat_axis=0, tiled=True)  74.6 us
    all_to_all x1, starting transfers between devices, per_device(): lax.all_to_all(outgoing, 'grp', split_axis=0, concat_axis=0, tiled=True)  19 us
    all_to_all x1, starting transfers between devices, per_device(): lax.all_to_all(kv_weight, 'tp', split_axis=1, concat_axis=0, tiled=True)  11.8 us
    gather x1, local copies, waits for them, and re-layouts, per_device(): outgoing = long_cache[0][order]  8.4 us
  transfers between devices with their start and end apart: 3, of which 3 were waited for; matrix products, arithmetic and copies ran while one was open for 7% of the time, Pallas kernels for 0%

commit v1 on v0

v1 whole, which is shorter than its diff:
```python
import jax
import jax.numpy as jnp
from jax import lax
from jax.sharding import PartitionSpec as P

HS = 128
ROPE_BASE = 1000000.0
masked_score = -1e30


def rotate(keys_raw, positions):
    half_dim = HS // 2
    freqs = jnp.power(jnp.float32(ROPE_BASE), -2.0 * jnp.arange(half_dim, dtype=jnp.float32) / HS)
    angles = positions.astype(jnp.float32)[..., None] * freqs
    cosine = jnp.cos(angles)
    sine = jnp.sin(angles)
    first_half = keys_raw[..., :half_dim]
    second_half = keys_raw[..., half_dim:]
    return jnp.concatenate(
        [first_half * cosine - second_half * sine, second_half * cosine + first_half * sine],
        axis=-1,
    )


def cached(query, cache, lengths):
    keys, values = cache[..., :HS], cache[..., HS:]
    scores = jnp.einsum("brd,bcd->brc", query, keys, preferred_element_type=jnp.float32) * HS**-0.5
    valid = jnp.arange(cache.shape[1], dtype=jnp.int32)[None, :] < lengths[:, None]
    scores = jnp.where(valid[:, None, :], scores, masked_score)
    top = jnp.max(scores, -1, keepdims=True)
    probs = jnp.exp(scores - top)
    total = jnp.sum(probs, -1, keepdims=True)
    mixed = jnp.einsum(
        "brc,bcd->brd", probs.astype(jnp.bfloat16), values, preferred_element_type=jnp.float32
    )
    return mixed / total, top + jnp.log(total)


def per_device(
    kv_weight, kv_bias, hidden_in, queries, res_cache, res_len, long_cache, long_len, long_dest
):
    steps, _, rows, width = hidden_in.shape
    groups = long_dest.shape[0]
    stay = rows - groups
    heads = queries.shape[3] // HS
    group = lax.axis_index("grp")

    part = jnp.dot(
        hidden_in.reshape(steps * rows, width), kv_weight, preferred_element_type=jnp.float32
    )
    kv = lax.psum_scatter(part, "tp", scatter_dimension=1, tiled=True)
    kv = (kv + kv_bias.astype(jnp.float32)).reshape(steps, rows, 2 * HS)

    matched = (long_dest == group).astype(jnp.int32)
    served = jnp.concatenate([res_len[0], jnp.sum(matched * long_len, axis=1)])
    positions = served[None, :] + jnp.arange(steps, dtype=jnp.int32)[:, None]
    new_keys = rotate(kv[..., :HS], positions).astype(jnp.bfloat16)
    new_values = kv[..., HS:].astype(jnp.bfloat16)

    query = queries[:, 0].reshape(steps, rows, heads, HS).transpose(1, 0, 2, 3)
    query = query.reshape(rows, steps * heads, HS)
    came = lax.all_to_all(query[stay:], "grp", split_axis=0, concat_axis=0, tiled=True)
    own_dest = lax.dynamic_index_in_dim(long_dest, group, 0, keepdims=False)
    own_long = lax.dynamic_index_in_dim(long_len, group, 0, keepdims=False)
    out, lse = cached(came[own_dest], long_cache[0], own_long)
    pick = jnp.argsort(own_dest)
    back = lax.all_to_all(out.astype(jnp.bfloat16)[pick], "grp", 0, 0, tiled=True)
    back_lse = lax.all_to_all(lse[pick], "grp", 0, 0, tiled=True)
    out_res, lse_res = cached(query[:stay], res_cache[0], res_len[0])
    old = jnp.concatenate([out_res, back.astype(jnp.float32)])
    old_lse = jnp.concatenate([lse_res, back_lse])

    scores = jnp.einsum("brd,tbd->brt", query, new_keys, preferred_element_type=jnp.float32)
    scores = scores * HS**-0.5
    step_of = jnp.arange(steps * heads, dtype=jnp.int32) // heads
    seen = jnp.arange(steps, dtype=jnp.int32)[None, :] <= step_of[:, None]
    scores = jnp.where(seen[None], scores, masked_score)
    top = jnp.maximum(jnp.max(scores, -1, keepdims=True), old_lse)
    probs = jnp.exp(scores - top)
    share = jnp.exp(old_lse - top)
    total = jnp.sum(probs, -1, keepdims=True) + share
    mixed = jnp.einsum(
        "brt,tbd->brd", (probs / total).astype(jnp.bfloat16), new_values,
        preferred_element_type=jnp.float32,
    )
    mixed = mixed + old * (share / total)
    mixed = mixed.astype(jnp.bfloat16).reshape(rows, steps, heads * HS).transpose(1, 0, 2)
    return mixed[:, None]


def solution(mesh):
    placed = (
        P("tp", None),
        P("tp"),
        P(None, "grp", None, "tp"),
        P(None, "grp", None, "tp"),
        P("grp", None, None, "tp"),
        P("grp", None),
        P("grp", None, None, "tp"),
        P(),
        P(),
    )
    return jax.shard_map(
        per_device,
        mesh=mesh,
        in_specs=placed,
        out_specs=P(None, "grp", None, "tp"),
        check_vma=False,
    )
```

time: 371 us -> 124 us (0.33)
  waiting for transfers between devices: 285 us -> 67.1 us
  local copies, waits for them, and re-layouts: 22.6 us -> 6.06 us
  starting transfers between devices: 30.8 us -> 17.5 us
    all_to_all x2 -> x3, waiting for transfers between devices: 175 us -> 14.7 us  [the longest x1 10.9 us: per_device(): lax.all_to_all(out.astype(jnp.bfloat16)[pick], 'grp', 0, 0, tiled=True)]
    all_gather x1 -> x0, waiting for transfers between devices: 109 us -> none  [per_device(): piece = lax.all_gather(hidden_in, 'tp', axis=3, tiled=True)]
    reduce_scatter x0 -> x1, waiting for transfers between devices: none -> 52.4 us  [per_device(): kv = lax.psum_scatter(part, 'tp', scatter_dimension=1, tiled=True)]
    all_to_all x2 -> x3, starting transfers between devices: 30.7 us -> 17.5 us  [the longest x1 10 us: per_device(): lax.all_to_all(query[stay:], 'grp', split_axis=0, concat_axis=0, tiled=True)]
    all_to_all x1 -> x0, local copies, waits for them, and re-layouts: 6.46 us -> none  [per_device(): lax.all_to_all(kv_weight, 'tp', split_axis=1, concat_axis=0, tiled=True)]
    gather x1 -> x3, local copies, waits for them, and re-layouts: 8.4 us -> 3.05 us  [the longest x1 1.29 us: per_device(): out.astype(jnp.bfloat16)[pick]]
    unnamed x14 -> x13, local copies, waits for them, and re-layouts: 6.48 us -> 1.14 us
    dot_general x9 -> x7, matrix products: 14.2 us -> 13.2 us  [the longest x1 4.42 us: per_device(): jnp.dot(hidden_in.reshape(steps * rows, width), kv_weight, preferred_elem...]
  transfers between devices with their start and end apart: 3 -> 4, of which waited for: 3 -> 3; matrix products, arithmetic and copies ran while one was open for 7% -> 17% of each run, Pallas kernels for 0% -> 0%
where the time goes in v1:
time: 124 us; the launch traced here: 123 us
  waiting for transfers between devices  67.1 us (54%)
  starting transfers between devices  17.5 us (14%)
  between operations  13.7 us (11%)
  matrix products  13.2 us (11%)
  local copies, waits for them, and re-layouts  6.06 us (5%)
  other arithmetic  5.14 us (4%)
    reduce_scatter x1, waiting for transfers between devices, per_device(): kv = lax.psum_scatter(part, 'tp', scatter_dimension=1, tiled=True)  52.4 us
    all_to_all x1, waiting for transfers between devices, per_device(): lax.all_to_all(out.astype(jnp.bfloat16)[pick], 'grp', 0, 0, tiled=True)  10.9 us
    all_to_all x1, starting transfers between devices, per_device(): lax.all_to_all(query[stay:], 'grp', split_axis=0, concat_axis=0, tiled=True)  10 us
    dot_general x1, matrix products, per_device(): jnp.dot(hidden_in.reshape(steps * rows, width), kv_weight, preferred_elem...  4.42 us
    dot_general x2, matrix products, cached(): jnp.einsum('brd,bcd->brc', query, keys, preferred_element_type=jnp.float32)  4.26 us
    all_to_all x1, starting transfers between devices, per_device(): lax.all_to_all(out.astype(jnp.bfloat16)[pick], 'grp', 0, 0, tiled=True)  3.85 us
    all_to_all x1, waiting for transfers between devices, per_device(): lax.all_to_all(query[stay:], 'grp', split_axis=0, concat_axis=0, tiled=True)  3.78 us
    dot_general x2, matrix products, cached(): jnp.einsum('brc,bcd->brd', probs.astype(jnp.bfloat16), values, preferred_...  3.66 us
  transfers between devices with their start and end apart: 4, of which 3 were waited for; matrix products, arithmetic and copies ran while one was open for 17% of the time, Pallas kernels for 0%

profile of v1, /device:TPU:1, one launch (start us, length us, event | category | flops | bytes accessed | tf_op | source)
XLA Modules:
  0.0 122.7 jit_solution(9516054067385187372)
XLA Ops:
  6.5 1.1 copy.24
  7.7 0.7 slice_bitcast_fusion
  8.5 10.0 %all-to-all-start = ((bf16[32,32,128]{2,1,0:T(8,128)(2,1)}), bf16[32,32,128]{2,1,0:T(8,128)(2,1)S(1)}, u32[]{:S(2)}, u32[]{:S(2)}) async-start(bf16[32,32,128]{2,1,0:T(8,128)(2,1)} %slice_bitcast_fusion), calls=%async_computation.1 | async-start | bytes 524288 | tf_op jit(solution)/shard_map/all_to_all | solution.py:62
  18.6 4.4 %fusion.59 = f32[192,2048]{1,0:T(8,128)} fusion(bf16[192,1024]{1,0:T(8,128)(2,1)S(1)} %bitcast.59, bf16[1024,2048]{1,0:T(8,128)(2,1)} %param.9), kind=kOutput, calls=%fused_computation.91 | convolution fusion | flops 805306368 | bytes 6160384 | tf_op jit(solution)/shard_map/dot_general | solution.py:48
  23.1 0.1 select_reduce_fusion
  23.2 1.6 %sort.17 = (s32[32]{0:T(128)}, s32[32]{0:T(128)S(1)}) sort(s32[32]{0:T(128)S(1)} %fusion.52, s32[32]{0:T(128)S(1)} %iota.46), dimensions={0}, to_apply=%region_7.8 | sort | flops 160 | bytes 512 | tf_op jit(solution)/shard_map/jit(argsort)/sort | solution.py:66
  24.9 0.1 iota_compare_fusion.1
  25.0 0.5 fusion.57
  25.4 0.3 fusion.31
  25.7 0.1 iota_compare_fusion
  25.8 0.1 pad_add_fusion
  25.9 0.1 add_convert_fusion
  26.0 3.8 %all-to-all-done = bf16[32,32,128]{2,1,0:T(8,128)(2,1)S(1)} async-done(((bf16[32,32,128]{2,1,0:T(8,128)(2,1)}), bf16[32,32,128]{2,1,0:T(8,128)(2,1)S(1)}, u32[]{:S(2)}, u32[]{:S(2)}) %all-to-all-start) | async-done | bytes 262176 | tf_op jit(solution)/shard_map/all_to_all | solution.py:62
  29.8 0.6 gather_fusion
  30.4 3.8 %fusion.4 = (f32[32,32]{1,0:T(8,128)S(1)}, f32[32,32,512]{2,1,0:T(8,128)S(1)}) fusion(pred[32,512]{1,0:T(8,128)(4,1)S(1)} %iota_compare_fusion, bf16[32,32,128]{2,1,0:T(8,128)(2,1)S(1)} %gather_fusion, bf16[32,512,256]{2,1,0:T(8,128)(2,1)} %bitcast.60), kind=kOutput, calls=%fused_computation.9 | convolution fusion | flops 135789568 | bytes 6574080 | tf_op jit(solution)/shard_map/brd,bcd->brc/dot_general | solution.py:27
  34.2 0.8 fusion.6
  35.0 3.3 %fusion.17 = bf16[32,32,128]{2,1,0:T(8,128)(2,1)S(1)} fusion(bf16[32,512,256]{2,1,0:T(8,128)(2,1)} %bitcast.61, f32[32,32,512]{2,1,0:T(8,128)S(1)} %get-tuple-element.14, f32[32,32]{1,0:T(8,128)S(1)} %get-tuple-element.13, pred[32,512]{1,0:T(8,128)(4,1)S(1)} %iota_compare_fusion, f32[32,32]{1,0:T(8,128)S(1)} %fusion.6), kind=kOutput, calls=%fused_computation.21 | convolution fusion | flops 136577024 | bytes 6578176 | tf_op jit(solution)/shard_map/brc,bcd->brd/dot_general | solution.py:33
  38.3 1.3 %gather_fusion.2 = bf16[32,32,128]{2,1,0:T(8,128)(2,1)} fusion(bf16[32,32,128]{2,1,0:T(8,128)(2,1)S(1)} %fusion.17, s32[1024]{0:T(1024)S(1)} %pad_clamp_fusion), kind=kCustom, calls=%fused_computation.2 | custom fusion | bytes 524416 | tf_op jit(solution)/shard_map/gather | solution.py:67
  39.6 3.9 %all-to-all-start.2 = ((bf16[32,32,128]{2,1,0:T(8,128)(2,1)}), bf16[32,32,128]{2,1,0:T(8,128)(2,1)S(1)}, u32[]{:S(2)}, u32[]{:S(2)}) async-start(bf16[32,32,128]{2,1,0:T(8,128)(2,1)} %gather_fusion.2), calls=%async_computation.3 | async-start | bytes 524288 | tf_op jit(solution)/shard_map/all_to_all | solution.py:67
  43.5 0.3 convolution_divide_fusion
  43.9 1.2 gather_fusion.1
  45.0 10.9 %all-to-all-done.2 = bf16[32,32,128]{2,1,0:T(8,128)(2,1)S(1)} async-done(((bf16[32,32,128]{2,1,0:T(8,128)(2,1)}), bf16[32,32,128]{2,1,0:T(8,128)(2,1)S(1)}, u32[]{:S(2)}, u32[]{:S(2)}) %all-to-all-start.2) | async-done | bytes 262176 | tf_op jit(solution)/shard_map/all_to_all | solution.py:67
  55.9 3.6 %all-to-all-start.1 = ((f32[32,32,1]{1,2,0:T(1,128)}), f32[32,32,1]{1,2,0:T(1,128)S(1)}, u32[]{:S(2)}, u32[]{:S(2)}) async-start(f32[32,32,1]{1,2,0:T(1,128)} %bitcast.15), calls=%async_computation.2 | async-start | bytes 32768 | tf_op jit(solution)/shard_map/all_to_all | solution.py:68
  59.6 52.4 %reduce-scatter.2.cloned.1.call-done = f32[192,256]{1,0:T(8,128)} async-done(((f32[192,2048]{1,0:T(8,128)}), f32[192,256]{1,0:T(8,128)}) %reduce-scatter.2.cloned.1.call-update) | async-done | bytes 196624 | tf_op jit(solution)/shard_map/reduce_scatter | solution.py:51
  112.0 0.9 broadcast_add_fusion
  113.0 0.1 fusion.56
  113.1 0.8 fusion.39
  113.9 0.4 fusion.58
  114.3 0.1 fusion.42
  114.5 0.4 fusion.7
  114.9 0.1 reshape.249
  115.0 0.9 copy.39
  (32 shorter events, 0.3 us)
Async XLA Ops:
  6.5 12.0 %copy-start = (bf16[4,1,48,1024]{3,2,1,0:T(8,128)(2,1)S(1)}, bf16[4,1,48,1024]{3,2,1,0:T(8,128)(2,1)}, u32[]{:S(2)}) copy-start(bf16[4,1,48,1024]{3,2,1,0:T(8,128)(2,1)} %param.11) | copy-start | bytes 1179652
  8.5 21.3 %all-to-all-start = ((bf16[32,32,128]{2,1,0:T(8,128)(2,1)}), bf16[32,32,128]{2,1,0:T(8,128)(2,1)S(1)}, u32[]{:S(2)}, u32[]{:S(2)}) async-start(bf16[32,32,128]{2,1,0:T(8,128)(2,1)} %slice_bitcast_fusion), calls=%async_computation.1 | async-start | bytes 524288 | tf_op jit(solution)/shard_map/all_to_all | solution.py:62
  18.5 93.6 %reduce-scatter.2.cloned.1.call-start = ((), (), s32[]{:S(2)}) async-start(), calls=%async_computation.4 | async-start | bytes 1769472 | tf_op jit(solution)/shard_map/reduce_scatter | solution.py:51
  18.5 4.5 %copy-start.1 = (s32[32,32]{1,0:T(8,128)S(1)}, s32[32,32]{1,0:T(8,128)}, u32[]{:S(2)}) copy-start(s32[32,32]{1,0:T(8,128)} %param.17) | copy-start | bytes 12292
  18.5 4.5 %copy-start.2 = (s32[32,32]{1,0:T(8,128)S(1)}, s32[32,32]{1,0:T(8,128)}, u32[]{:S(2)}) copy-start(s32[32,32]{1,0:T(8,128)} %param.16) | copy-start | bytes 12292
  18.6 6.3 %copy-start.3 = (s32[1,16]{1,0:T(1,128)S(1)}, s32[1,16]{1,0:T(1,128)}, u32[]{:S(2)}) copy-start(s32[1,16]{1,0:T(1,128)} %param.14) | copy-start | bytes 196
  18.6 6.4 %copy-start.4 = (bf16[1,16,128,256]{3,2,1,0:T(8,128)(2,1)S(1)}, bf16[1,16,128,256]{3,2,1,0:T(8,128)(2,1)}, u32[]{:S(2)}) copy-start(bf16[1,16,128,256]{3,2,1,0:T(8,128)(2,1)} %param.13) | copy-start | bytes 3145732
  35.0 8.5 %copy-start.5 = (bf16[256]{0:T(256)(128)(2,1)S(1)}, bf16[256]{0:T(256)(128)(2,1)}, u32[]{:S(2)}) copy-start(bf16[256]{0:T(256)(128)(2,1)} %param.10) | copy-start | bytes 1540
  39.6 16.3 %all-to-all-start.2 = ((bf16[32,32,128]{2,1,0:T(8,128)(2,1)}), bf16[32,32,128]{2,1,0:T(8,128)(2,1)S(1)}, u32[]{:S(2)}, u32[]{:S(2)}) async-start(bf16[32,32,128]{2,1,0:T(8,128)(2,1)} %gather_fusion.2), calls=%async_computation.3 | async-start | bytes 524288 | tf_op jit(solution)/shard_map/all_to_all | solution.py:67
  55.9 58.4 %all-to-all-start.1 = ((f32[32,32,1]{1,2,0:T(1,128)}), f32[32,32,1]{1,2,0:T(1,128)S(1)}, u32[]{:S(2)}, u32[]{:S(2)}) async-start(f32[32,32,1]{1,2,0:T(1,128)} %bitcast.15), calls=%async_computation.2 | async-start | bytes 32768 | tf_op jit(solution)/shard_map/all_to_all | solution.py:68
Sparse Core Ops, SparseCore 0:
  23.4 88.6 reduce-scatter.1
